TPU v7x, 32 devices: a whole 2x2x4 slice. The times are simulated.
32 devices in a mesh: groups: 2 (over x), seq: 8 (over z, y), tp: 2 (over core).
Axes of the slice: x: 2, y: 2, z: 4, core: 2. Of those that a mesh axis runs over, the one named last changes fastest.
Arguments:
- queries: bfloat16 [4096, 8192], P(('groups', 'seq', 'tp')), parts along dimension 0, may hold values from -10 to 10
- keys: bfloat16 [4096, 1024], P(('groups', 'seq', 'tp')), parts along dimension 0, may hold values from -10 to 10
- values: bfloat16 [4096, 1024], P(('groups', 'seq', 'tp')), parts along dimension 0, may hold values from -6 to 6
- vertical_blocks: int32 [64, 2], replicated, may hold values from 0 to 15, as said below
- vertical_count: int32 [64], replicated, may hold values from 1 to 2, as said below
- slash_offsets: int32 [64, 2], replicated, may hold values from 1 to 15, as said below
- slash_count: int32 [64], replicated, may hold values from 1 to 2, as said below
Outputs:
- attention: bfloat16 [4096, 8192], P(('groups', 'seq', 'tp')), parts along dimension 0
There are 2 independent parts, one for each index of `groups`. A program takes and returns all parts, laid end to end along the dimension named above; an argument that names none is the same for every part. Nothing has to cross between parts.
Inputs may be any that keep to these rules, and one draw needn't show every extreme that they name: `vertical_blocks`: the 2 entries of one head are distinct. `vertical_count`: some head uses all 2 entries. `slash_offsets`: the 2 entries of one head are distinct. `slash_count`: some head uses all 2 entries.
All inputs are finite; a program needn't handle non-finite values.
Results may differ from a plain program's by a relative error of at most 0.0037.
Values may be sent and summed in bfloat16 or wider, within the bound.
A program may use at most 128 MiB of HBM per device.

v0:
```python
import jax
import jax.numpy as jnp
import numpy as np
from jax import lax
from jax.sharding import PartitionSpec as P

QUERY_HEADS = 64
KEY_VALUE_HEADS = 8
HEAD_SIZE = 128
MASK_BLOCK_SIZE = 128


def head_attend(
    query_blocks,
    block_index,
    row_offset,
    key_blocks,
    value_blocks,
    verticals,
    vertical_live,
    slash_list,
    slash_live,
):
    query_rows = query_blocks.shape[1]
    scaling = query_blocks.shape[2] ** (-0.5)
    total_block_count = key_blocks.shape[0]
    block_width = key_blocks.shape[1]
    block_total = block_index.shape[0]
    vertical_entries = jnp.arange(verticals.shape[0])
    slash_entries = jnp.arange(slash_list.shape[0])
    member = jnp.any(
        (jnp.arange(total_block_count)[:, None] == verticals[None, :])
        & (vertical_entries < vertical_live)[None, :],
        axis=1,
    )
    vertical_active = (block_index[:, None] > verticals[None, :]) & (
        vertical_entries < vertical_live
    )[None, :]
    targets = block_index[:, None] - slash_list[None, :]
    safe_targets = jnp.clip(targets, 0, total_block_count - 1)
    slash_active = (
        (targets >= 0)
        & (slash_entries < slash_live)[None, :]
        & jnp.logical_not(jnp.take(member, safe_targets))
    )
    tile_index = jnp.concatenate(
        [
            block_index[:, None],
            jnp.broadcast_to(verticals[None, :], (block_total, verticals.shape[0])),
            safe_targets,
        ],
        axis=1,
    )
    tile_active = jnp.concatenate(
        [jnp.ones((block_total, 1), bool), vertical_active, slash_active], axis=1
    )
    tile_keys = jnp.take(key_blocks, tile_index, axis=0)
    tile_values = jnp.take(value_blocks, tile_index, axis=0)
    scores = (
        jnp.einsum("nqd,ntkd->nqtk", query_blocks, tile_keys, preferred_element_type=jnp.float32)
        * scaling
    )
    query_pos = row_offset + jnp.arange(query_rows)
    causal = query_pos[:, None] >= jnp.arange(block_width)[None, :]
    off_diagonal = (jnp.arange(tile_index.shape[1]) > 0)[None, None, :, None]
    allowed = tile_active[:, None, :, None] & (causal[None, :, None, :] | off_diagonal)
    scores = jnp.where(allowed, scores, -jnp.inf)
    peak = jnp.max(scores, axis=(2, 3))
    weights = jnp.exp(scores - peak[:, :, None, None])
    total = jnp.sum(weights, axis=(2, 3))
    rounded = weights.astype(jnp.bfloat16)
    numerator = jnp.einsum(
        "nqtk,ntkd->nqd", rounded, tile_values, preferred_element_type=jnp.float32
    )
    return (numerator / total[..., None]).astype(jnp.bfloat16)


def shards(queries, keys, values, vertical_blocks, vertical_count, slash_offsets, slash_count):
    local_token_count = queries.shape[0]
    seq_ranks = lax.axis_size("seq")
    core_count = lax.axis_size("tp")
    core_index = lax.axis_index("tp")
    rank_index = lax.axis_index("seq")
    heads_rank = QUERY_HEADS // seq_ranks
    heads_per_group = QUERY_HEADS // KEY_VALUE_HEADS
    kv_rank = max(1, heads_rank // heads_per_group)
    query_width = heads_rank * HEAD_SIZE
    kv_width = kv_rank * HEAD_SIZE
    key_value_lookup = (
        (
            np.arange(seq_ranks)[:, None] * heads_rank // heads_per_group
            + np.arange(kv_rank)[None, :]
        )
        .reshape(-1)
        .astype(np.int32)
    )
    key_selection = jnp.take(
        keys.reshape(local_token_count, KEY_VALUE_HEADS, HEAD_SIZE), key_value_lookup, axis=1
    ).reshape(local_token_count, seq_ranks * kv_width)
    value_selection = jnp.take(
        values.reshape(local_token_count, KEY_VALUE_HEADS, HEAD_SIZE), key_value_lookup, axis=1
    ).reshape(local_token_count, seq_ranks * kv_width)
    per_shard = local_token_count // MASK_BLOCK_SIZE
    total_block_count = seq_ranks * core_count * per_shard
    query_got, key_portion, value_part = (
        lax.all_to_all(queries, "seq", split_axis=1, concat_axis=0, tiled=True),
        lax.all_to_all(key_selection, "seq", split_axis=1, concat_axis=0, tiled=True),
        lax.all_to_all(value_selection, "seq", split_axis=1, concat_axis=0, tiled=True),
    )
    key_rows, value_rows = (
        lax.all_gather(
            key_portion.reshape(seq_ranks, 1, local_token_count, kv_width), "tp", axis=1, tiled=True
        ),
        lax.all_gather(
            value_part.reshape(seq_ranks, 1, local_token_count, kv_width), "tp", axis=1, tiled=True
        ),
    )
    local_blocks = seq_ranks * per_shard
    query_rows = MASK_BLOCK_SIZE
    row_offset = 0
    block_order = jnp.arange(local_blocks, dtype=jnp.int32)
    block_index = (
        block_order // per_shard * core_count + core_index
    ) * per_shard + block_order % per_shard
    key_blocks_all = key_rows.reshape(total_block_count, MASK_BLOCK_SIZE, kv_rank, HEAD_SIZE)
    value_blocks_all = value_rows.reshape(total_block_count, MASK_BLOCK_SIZE, kv_rank, HEAD_SIZE)
    query_all = query_got.reshape(local_blocks, query_rows, heads_rank, HEAD_SIZE)
    results = []
    for head_slot in range(heads_rank):
        head = rank_index * heads_rank + head_slot
        kv_slot = head // heads_per_group - rank_index * heads_rank // heads_per_group
        key_blocks = lax.dynamic_index_in_dim(key_blocks_all, kv_slot, 2, False)
        value_blocks = lax.dynamic_index_in_dim(value_blocks_all, kv_slot, 2, False)
        results.append(
            head_attend(
                query_all[:, :, head_slot],
                block_index,
                row_offset,
                key_blocks,
                value_blocks,
                lax.dynamic_index_in_dim(vertical_blocks, head, 0, False),
                lax.dynamic_index_in_dim(vertical_count, head, 0, False),
                lax.dynamic_index_in_dim(slash_offsets, head, 0, False),
                lax.dynamic_index_in_dim(slash_count, head, 0, False),
            )
        )
    attended = jnp.stack(results, axis=2).reshape(local_blocks * query_rows, query_width)
    return lax.all_to_all(attended, "seq", split_axis=0, concat_axis=1, tiled=True)


def solution(mesh):
    return jax.shard_map(
        shards,
        mesh=mesh,
        in_specs=(
            P(("groups", "seq", "tp"), None),
            P(("groups", "seq", "tp"), None),
            P(("groups", "seq", "tp"), None),
            P(),
            P(),
            P(),
            P(),
        ),
        out_specs=P(("groups", "seq", "tp"), None),
        check_vma=False,
    )
```

profile of v0, /device:TPU:0, one launch (start us, length us, event | category | flops | bytes accessed | tf_op | source)
XLA Modules:
  0.0 186.8 jit_solution(7677651605231621368)
XLA Ops:
  0.0 1.1 copy.79
  1.3 1.1 copy.75
  4.8 7.3 %all-to-all-start = ((bf16[128,8,128]{2,0,1:T(8,128)(2,1)}), bf16[128,8,128]{2,0,1:T(8,128)(2,1)S(1)}, u32[]{:S(2)}, u32[]{:S(2)}) async-start(bf16[128,8,128]{2,0,1:T(8,128)(2,1)} %get-tuple-element.123), calls=%async_computation | async-start | bytes 524288 | tf_op jit(solution)/shard_map/all_to_all | solution.py:107
  19.0 2.1 %all-to-all-done = bf16[128,8,128]{2,0,1:T(8,128)(2,1)S(1)} async-done(((bf16[128,8,128]{2,0,1:T(8,128)(2,1)}), bf16[128,8,128]{2,0,1:T(8,128)(2,1)S(1)}, u32[]{:S(2)}, u32[]{:S(2)}) %all-to-all-start) | async-done | bytes 262176 | tf_op jit(solution)/shard_map/all_to_all | solution.py:107
  21.1 4.0 %all-to-all-start.2 = ((bf16[128,8,128]{2,0,1:T(8,128)(2,1)}), bf16[128,8,128]{2,0,1:T(8,128)(2,1)S(1)}, u32[]{:S(2)}, u32[]{:S(2)}) async-start(bf16[128,8,128]{2,0,1:T(8,128)(2,1)} %get-tuple-element.122), calls=%async_computation.2 | async-start | bytes 524288 | tf_op jit(solution)/shard_map/all_to_all | solution.py:108
  25.0 2.4 %copy.77 = bf16[128,8192]{0,1:T(8,128)(2,1)} copy(bf16[128,8192]{1,0:T(8,128)(2,1)S(1)} %copy-done.7) | data formatting | bytes 4194304 | tf_op args[0]
  27.8 5.7 %all-to-all-done.2 = bf16[128,8,128]{2,0,1:T(8,128)(2,1)S(1)} async-done(((bf16[128,8,128]{2,0,1:T(8,128)(2,1)}), bf16[128,8,128]{2,0,1:T(8,128)(2,1)S(1)}, u32[]{:S(2)}, u32[]{:S(2)}) %all-to-all-start.2) | async-done | bytes 262176 | tf_op jit(solution)/shard_map/all_to_all | solution.py:108
  33.5 4.3 %all-to-all-start.1 = ((bf16[128,8,1024]{0,2,1:T(8,128)(2,1)}), bf16[128,8,1024]{0,2,1:T(8,128)(2,1)}, u32[]{:S(2)}, u32[]{:S(2)}) async-start(bf16[128,8,1024]{0,2,1:T(8,128)(2,1)} %bitcast.7), calls=%async_computation.1 | async-start | bytes 4194304 | tf_op jit(solution)/shard_map/all_to_all | solution.py:106
  51.1 2.2 %all-gather = bf16[8,256,128]{2,1,0:T(8,128)(2,1)S(1)} all-gather(bf16[8,128,128]{2,1,0:T(8,128)(2,1)S(1)} %bitcast.293), channel_id=2, replica_groups=mesh['groups'=2,'seq'=8,'tp'=2] {'tp'}, dimensions={1}, use_global_device_ids=true | all-gather | bytes 786432 | tf_op jit(solution)/shard_map/all_gather | solution.py:111
  53.3 1.8 gather_fusion.2
  55.1 2.2 %all-gather.1 = bf16[8,256,128]{2,1,0:T(8,128)(2,1)S(1)} all-gather(bf16[8,128,128]{2,1,0:T(8,128)(2,1)S(1)} %bitcast.294), channel_id=3, replica_groups=mesh['groups'=2,'seq'=8,'tp'=2] {'tp'}, dimensions={1}, use_global_device_ids=true | all-gather | bytes 786432 | tf_op jit(solution)/shard_map/all_gather | solution.py:114
  58.1 1.8 gather_fusion.6
  60.0 1.9 %gather_fusion.7 = bf16[40,128,128]{2,1,0:T(8,128)(2,1)} fusion(bf16[16,128,128]{2,1,0:T(8,128)(2,1)S(1)} %bitcast.268, s32[1024]{0:T(1024)S(1)} %pad_clamp_fusion.13), kind=kCustom, calls=%fused_computation.13.clone | custom fusion | bytes 2621600 | tf_op jit(solution)/shard_map/jit(_take)/gather | solution.py:58
  61.9 1.9 %gather_fusion.9 = bf16[40,128,128]{2,1,0:T(8,128)(2,1)} fusion(bf16[16,128,128]{2,1,0:T(8,128)(2,1)S(1)} %bitcast.261, s32[1024]{0:T(1024)S(1)} %pad_clamp_fusion.11), kind=kCustom, calls=%fused_computation.14.clone | custom fusion | bytes 2621600 | tf_op jit(solution)/shard_map/jit(_take)/gather | solution.py:57
  63.8 1.9 gather_fusion.10
  65.6 1.9 %gather_fusion.12 = bf16[40,128,128]{2,1,0:T(8,128)(2,1)} fusion(bf16[16,128,128]{2,1,0:T(8,128)(2,1)S(1)} %bitcast.262, s32[1024]{0:T(1024)S(1)} %pad_clamp_fusion.9), kind=kCustom, calls=%fused_computation.16.clone | custom fusion | bytes 2621600 | tf_op jit(solution)/shard_map/jit(_take)/gather | solution.py:57
  67.6 1.9 %gather_fusion.13 = bf16[40,128,128]{2,1,0:T(8,128)(2,1)} fusion(bf16[16,128,128]{2,1,0:T(8,128)(2,1)S(1)} %bitcast.270, s32[1024]{0:T(1024)S(1)} %pad_clamp_fusion.9), kind=kCustom, calls=%fused_computation.17.clone | custom fusion | bytes 2621600 | tf_op jit(solution)/shard_map/jit(_take)/gather | solution.py:58
  69.4 1.9 %gather_fusion.15 = bf16[40,128,128]{2,1,0:T(8,128)(2,1)} fusion(bf16[16,128,128]{2,1,0:T(8,128)(2,1)S(1)} %bitcast.263, s32[1024]{0:T(1024)S(1)} %pad_clamp_fusion.7), kind=kCustom, calls=%fused_computation.18.clone | custom fusion | bytes 2621600 | tf_op jit(solution)/shard_map/jit(_take)/gather | solution.py:57
  71.3 1.9 gather_fusion.16
  73.2 1.9 %gather_fusion.18 = bf16[40,128,128]{2,1,0:T(8,128)(2,1)} fusion(bf16[16,128,128]{2,1,0:T(8,128)(2,1)S(1)} %bitcast.264, s32[1024]{0:T(1024)S(1)} %pad_clamp_fusion.5), kind=kCustom, calls=%fused_computation.20.clone | custom fusion | bytes 2621600 | tf_op jit(solution)/shard_map/jit(_take)/gather | solution.py:57
  75.1 1.9 %gather_fusion.19 = bf16[40,128,128]{2,1,0:T(8,128)(2,1)} fusion(bf16[16,128,128]{2,1,0:T(8,128)(2,1)S(1)} %bitcast.272, s32[1024]{0:T(1024)S(1)} %pad_clamp_fusion.5), kind=kCustom, calls=%fused_computation.21.clone | custom fusion | bytes 2621600 | tf_op jit(solution)/shard_map/jit(_take)/gather | solution.py:58
  77.0 1.8 gather_fusion.21
  78.8 1.9 %gather_fusion.22 = bf16[40,128,128]{2,1,0:T(8,128)(2,1)} fusion(bf16[16,128,128]{2,1,0:T(8,128)(2,1)S(1)} %bitcast.273, s32[1024]{0:T(1024)S(1)} %pad_clamp_fusion.3), kind=kCustom, calls=%fused_computation.23.clone | custom fusion | bytes 2621600 | tf_op jit(solution)/shard_map/jit(_take)/gather | solution.py:58
  80.7 1.8 gather_fusion.24
  82.5 1.9 %gather_fusion.25 = bf16[40,128,128]{2,1,0:T(8,128)(2,1)} fusion(bf16[16,128,128]{2,1,0:T(8,128)(2,1)S(1)} %bitcast.274, s32[1024]{0:T(1024)S(1)} %pad_clamp_fusion.1), kind=kCustom, calls=%fused_computation.25.clone | custom fusion | bytes 2621600 | tf_op jit(solution)/shard_map/jit(_take)/gather | solution.py:58
  84.4 1.4 copy.81
  85.9 1.5 copy.84
  87.4 1.5 copy.87
  88.8 1.5 copy.90
  90.3 1.5 copy.93
  91.8 1.4 copy.96
  93.2 1.4 copy.99
  94.6 1.0 copy.102
  95.6 2.0 %fusion.338 = (f32[8,128]{1,0:T(8,128)S(1)}, f32[8,128,5,128]{1,3,2,0:T(8,128)S(1)}) fusion(bf16[8,128,8,128]{1,3,2,0:T(8,128)(2,1)} %bitcast.9, bf16[8,5,128,128]{3,2,1,0:T(8,128)(2,1)} %bitcast.292, pred[8,5]{1,0:T(8,128)(4,1)S(1)} %get-tuple-element.50, pred[128,5,128]{0,2,1:T(8,128)(4,1)S(1)} %broadcast_or_fusion, pred[8,5]{1,0:T(8,128)(4,1)S(1)} %get-tuple-element.75), kind=kOutput, calls=%fused_computation.349 | convolution fusion | flops 171047936 | bytes 4280400 | tf_op jit(solution)/shard_map/nqd,ntkd->nqtk/dot_general | solution.py:60
  98.0 0.9 copy-done.21
  100.3 1.7 fusion.339
  102.3 0.9 copy-done.19
  103.3 1.7 fusion.340
  105.3 0.9 copy-done.18
  106.2 1.7 fusion.341
  109.2 1.7 fusion.342
  111.3 0.9 copy-done.16
  112.2 1.7 fusion.343
  115.2 1.7 fusion.344
  118.2 1.7 fusion.345
  125.1 1.1 fusion.187
  129.7 54.2 %all_to_all.61 = bf16[8,128,1024]{1,2,0:T(8,128)(2,1)S(1)} all-to-all(bf16[8,128,1024]{1,2,0:T(8,128)(2,1)S(1)} %bitcast.275), channel_id=1, replica_groups=mesh['groups'=2,'seq'=8,'tp'=2] {'seq'}, dimensions={0} | all-to-all | bytes 4194304 | tf_op jit(solution)/shard_map/all_to_all | solution.py:148
  183.9 2.9 %copy.105 = bf16[128,8192]{1,0:T(8,128)(2,1)} copy(bf16[128,8192]{0,1:T(8,128)(2,1)S(1)} %bitcast.276) | data formatting | bytes 4194304 | tf_op jit(solution)/shard_map/all_to_all | solution.py:148
  (169 shorter events, 38.9 us)
Async XLA Ops:
  2.7 9.5 %copy-start.24 = (s32[64]{0:T(128)S(1)}, s32[64]{0:T(128)}, u32[]{:S(2)}) copy-start(s32[64]{0:T(128)} %param.20) | copy-start | bytes 772
  2.7 9.5 %copy-start.25 = (s32[64]{0:T(128)S(1)}, s32[64]{0:T(128)}, u32[]{:S(2)}) copy-start(s32[64]{0:T(128)} %param.18) | copy-start | bytes 772
  2.7 10.9 %copy-start.22 = (s32[64,2]{0,1:T(2,128)S(1)}, s32[64,2]{0,1:T(2,128)}, u32[]{:S(2)}) copy-start(s32[64,2]{0,1:T(2,128)} %param.17) | copy-start | bytes 1540
  2.7 10.9 %copy-start.23 = (s32[64,2]{0,1:T(2,128)S(1)}, s32[64,2]{0,1:T(2,128)}, u32[]{:S(2)}) copy-start(s32[64,2]{0,1:T(2,128)} %param.19) | copy-start | bytes 1540
  3.9 21.1 %copy-start.7 = (bf16[128,8192]{1,0:T(8,128)(2,1)S(1)}, bf16[128,8192]{1,0:T(8,128)(2,1)}, u32[]{:S(2)}) copy-start(bf16[128,8192]{1,0:T(8,128)(2,1)} %param.14) | copy-start | bytes 6291460
  4.8 16.2 %all-to-all-start = ((bf16[128,8,128]{2,0,1:T(8,128)(2,1)}), bf16[128,8,128]{2,0,1:T(8,128)(2,1)S(1)}, u32[]{:S(2)}, u32[]{:S(2)}) async-start(bf16[128,8,128]{2,0,1:T(8,128)(2,1)} %get-tuple-element.123), calls=%async_computation | async-start | bytes 524288 | tf_op jit(solution)/shard_map/all_to_all | solution.py:107
  21.1 12.5 %all-to-all-start.2 = ((bf16[128,8,128]{2,0,1:T(8,128)(2,1)}), bf16[128,8,128]{2,0,1:T(8,128)(2,1)S(1)}, u32[]{:S(2)}, u32[]{:S(2)}) async-start(bf16[128,8,128]{2,0,1:T(8,128)(2,1)} %get-tuple-element.122), calls=%async_computation.2 | async-start | bytes 524288 | tf_op jit(solution)/shard_map/all_to_all | solution.py:108
  33.5 62.1 %all-to-all-start.1 = ((bf16[128,8,1024]{0,2,1:T(8,128)(2,1)}), bf16[128,8,1024]{0,2,1:T(8,128)(2,1)}, u32[]{:S(2)}, u32[]{:S(2)}) async-start(bf16[128,8,1024]{0,2,1:T(8,128)(2,1)} %bitcast.7), calls=%async_computation.1 | async-start | bytes 4194304 | tf_op jit(solution)/shard_map/all_to_all | solution.py:106
  84.4 1.4 copy-start
  85.9 1.5 copy-start.1
  87.4 1.5 copy-start.2
  88.8 1.5 copy-start.3
  90.3 1.5 copy-start.4
  91.8 1.4 copy-start.5
  93.2 1.4 copy-start.6
  97.7 1.3 copy-start.21
  99.0 1.3 copy-start.20
  101.9 1.3 copy-start.19
  104.9 1.3 copy-start.18
  107.9 1.3 copy-start.17
  110.9 1.3 copy-start.16
  113.9 1.3 copy-start.15
  116.9 1.3 copy-start.13
  119.8 1.3 copy-start.14
  121.2 1.3 copy-start.12
  122.5 1.3 copy-start.11
  123.8 1.3 copy-start.10
  125.1 1.3 copy-start.9
  126.4 1.3 copy-start.8
where the time goes:
time: 188 us; the launch traced here: 187 us
  local copies, waits for them, and re-layouts  68.2 us (36%)
  blocking collectives  58.6 us (31%)
  matrix products  20.6 us (11%)
  starting transfers between devices  15.6 us (8%)
  other arithmetic  15.4 us (8%)
  waiting for transfers between devices  7.75 us (4%)
    all_to_all x1, blocking collectives, shards(): lax.all_to_all(attended, 'seq', split_axis=0, concat_axis=1, tiled=True)  54.2 us
    gather x16, local copies, waits for them, and re-layouts, head_attend(): tile_values = jnp.take(value_blocks, tile_index, axis=0)  25.1 us
    gather x8, local copies, waits for them, and re-layouts, head_attend(): tile_keys = jnp.take(key_blocks, tile_index, axis=0)  15 us
    unnamed x55, local copies, waits for them, and re-layouts  14.9 us
    dot_general x8, matrix products, head_attend(): jnp.einsum('nqd,ntkd->nqtk', query_blocks, tile_keys, preferred_element_t...  13.6 us
    all_to_all x1, starting transfers between devices, shards(): lax.all_to_all(key_selection, 'seq', split_axis=1, concat_axis=0, tiled=T...  7.31 us
    dot_general x8, matrix products, head_attend(): jnp.einsum('nqtk,ntkd->nqd', rounded, tile_values, preferred_element_type...  6.98 us
    gather x16, local copies, waits for them, and re-layouts, head_attend(): jnp.take(member, safe_targets)  6.08 us
  transfers between devices with their start and end apart: 3, of which 2 were waited for; matrix products, arithmetic and copies ran while one was open for 34% of the time, Pallas kernels for 0%

commit v1 on v0

v1 whole, which is shorter than its diff:
```python
import functools
import math

import jax
import jax.numpy as jnp
from jax import lax
from jax.experimental import pallas as pl
from jax.experimental.pallas import tpu as pltpu
from jax.sharding import PartitionSpec as P

HEAD_SIZE = 128
BLOCK = 128


def attend(q, block, head, load_key, load_value, vb, vc, so, sc, causal):
    nv, ns = vb.shape[1], so.shape[1]
    factor = HEAD_SIZE**-0.5 * math.log2(math.e)
    count_v, count_s = vc[head], sc[head]
    index, live = [block], []
    verticals = [vb[head, e] for e in range(nv)]
    for e in range(nv):
        index.append(verticals[e])
        live.append(jnp.logical_and(e < count_v, verticals[e] < block))
    for e in range(ns):
        target = block - so[head, e]
        ok = jnp.logical_and(e < count_s, target >= 0)
        for f in range(nv):
            taken = jnp.logical_and(f < count_v, verticals[f] == target)
            ok = jnp.logical_and(ok, jnp.logical_not(taken))
        index.append(jnp.maximum(target, 0))
        live.append(ok)
    keys = jnp.concatenate([load_key(t) for t in index], axis=0)
    scores = lax.dot_general(
        q, keys, (((1,), (1,)), ((), ())), preferred_element_type=jnp.float32
    )
    tiles = [jnp.where(causal, scores[:, :BLOCK], -jnp.inf)]
    for t, ok in enumerate(live):
        bias = jnp.where(ok, 0.0, -jnp.inf).astype(jnp.float32)
        tiles.append(scores[:, (t + 1) * BLOCK : (t + 2) * BLOCK] + bias)
    highest = functools.reduce(jnp.maximum, tiles)
    peak = jnp.max(highest, axis=1, keepdims=True) * factor
    weights = [jnp.exp2(t * factor - peak) for t in tiles]
    total = jnp.sum(functools.reduce(jnp.add, weights), axis=1, keepdims=True)
    rounded = jnp.concatenate([w.astype(jnp.bfloat16) for w in weights], axis=1)
    vals = jnp.concatenate([load_value(t) for t in index], axis=0)
    numerator = jnp.dot(rounded, vals, preferred_element_type=jnp.float32)
    return (numerator / total).astype(jnp.bfloat16)


def kernel(per_group, vb, vc, so, sc, q_ref, k_ref, v_ref, o_ref):
    rank = lax.axis_index("seq") * lax.axis_size("tp") + lax.axis_index("tp")
    group = pl.program_id(0)
    per_shard = q_ref.shape[0] // BLOCK
    rows = lax.broadcasted_iota(jnp.int32, (BLOCK, BLOCK), 0)
    causal = rows >= lax.broadcasted_iota(jnp.int32, (BLOCK, BLOCK), 1)
    for b in range(per_shard):
        span = slice(b * BLOCK, (b + 1) * BLOCK)
        for slot in range(per_group):
            cols = slice(slot * HEAD_SIZE, (slot + 1) * HEAD_SIZE)
            o_ref[span, cols] = attend(
                q_ref[span, cols],
                rank * per_shard + b,
                group * per_group + slot,
                lambda t: k_ref[pl.ds(pl.multiple_of(t * BLOCK, BLOCK), BLOCK), :],
                lambda t: v_ref[pl.ds(pl.multiple_of(t * BLOCK, BLOCK), BLOCK), :],
                vb, vc, so, sc, causal,
            )


def shards(queries, keys, values, vertical_blocks, vertical_count, slash_offsets, slash_count):
    heads = vertical_count.shape[0]
    groups = keys.shape[1] // HEAD_SIZE
    per_group = heads // groups
    tokens = queries.shape[0]
    all_keys = lax.all_gather(keys, ("seq", "tp"), axis=0, tiled=True)
    all_values = lax.all_gather(values, ("seq", "tp"), axis=0, tiled=True)
    smem = pl.BlockSpec(memory_space=pltpu.SMEM)
    length = all_keys.shape[0]
    return pl.pallas_call(
        functools.partial(kernel, per_group),
        grid=(groups,),
        in_specs=[smem] * 4
        + [
            pl.BlockSpec((tokens, per_group * HEAD_SIZE), lambda g: (0, g)),
            pl.BlockSpec((length, HEAD_SIZE), lambda g: (0, g)),
            pl.BlockSpec((length, HEAD_SIZE), lambda g: (0, g)),
        ],
        out_specs=pl.BlockSpec((tokens, per_group * HEAD_SIZE), lambda g: (0, g)),
        out_shape=jax.ShapeDtypeStruct(queries.shape, jnp.bfloat16),
        compiler_params=pltpu.CompilerParams(vmem_limit_bytes=48 * 1024 * 1024),
    )(vertical_blocks, vertical_count, slash_offsets, slash_count, queries, all_keys, all_values)


def solution(mesh):
    rows = P(("groups", "seq", "tp"), None)
    return jax.shard_map(
        shards,
        mesh=mesh,
        in_specs=(rows, rows, rows, P(), P(), P(), P()),
        out_specs=rows,
        check_vma=False,
    )
```

time: 188 us -> 147 us (0.78)
  waiting for transfers between devices: 7.75 us -> 106 us
  local copies, waits for them, and re-layouts: 68.2 us -> 4.44 us
  blocking collectives: 58.6 us -> 0 us
  Pallas kernels: 0 us -> 23.5 us
  matrix products: 20.6 us -> 0 us
  starting transfers between devices: 15.6 us -> 0.04 us
  other arithmetic: 15.4 us -> 0 us
  between operations: 0.71 us -> 13.4 us
    all_gather x0 -> x2, waiting for transfers between devices: none -> 104 us  [the longest x1 53.1 us: shards(): all_keys = lax.all_gather(keys, ('seq', 'tp'), axis=0, tiled=True)]
    all_to_all x1 -> x0, blocking collectives: 54.2 us -> none  [shards(): lax.all_to_all(attended, 'seq', split_axis=0, concat_axis=1, tiled=True)]
    gather x42 -> x0, local copies, waits for them, and re-layouts: 47.4 us -> none  [the longest x16 25.1 us: head_attend(): tile_values = jnp.take(value_blocks, tile_index, axis=0)]
    pallas_call x0 -> x1, Pallas kernels: none -> 23.5 us  [shards(): pl.pallas_call(functools.partial(kernel, per_group), grid=(groups,), in_s...]
    dot_general x16 -> x0, matrix products: 20.6 us -> none  [the longest x8 13.6 us: head_attend(): jnp.einsum('nqd,ntkd->nqtk', query_blocks, tile_keys, preferred_element_t...]
    all_to_all x3 -> x0, starting transfers between devices: 15.6 us -> none  [the longest x1 7.31 us: shards(): lax.all_to_all(key_selection, 'seq', split_axis=1, concat_axis=0, tiled=T...]
    unnamed x55 -> x8, local copies, waits for them, and re-layouts: 14.9 us -> 4.44 us
    lt x16 -> x0, other arithmetic: 9.99 us -> none  [the longest x8 5.09 us: head_attend(): vertical_entries < vertical_live]
  transfers between devices with their start and end apart: 3 -> 2, of which waited for: 2 -> 2; matrix products, arithmetic and copies ran while one was open for 34% -> 1% of each run, Pallas kernels for 0% -> 0%
where the time goes in v1:
time: 147 us
  waiting for transfers between devices  106 us (72%)
  Pallas kernels  23.5 us (16%)
  between operations  13.4 us (9%)
  local copies, waits for them, and re-layouts  4.44 us (3%)
    all_gather x1, waiting for transfers between devices, shards(): all_keys = lax.all_gather(keys, ('seq', 'tp'), axis=0, tiled=True)  53.1 us
    all_gather x1, waiting for transfers between devices, shards(): all_values = lax.all_gather(values, ('seq', 'tp'), axis=0, tiled=True)  51.1 us
    pallas_call x1, Pallas kernels, shards(): pl.pallas_call(functools.partial(kernel, per_group), grid=(groups,), in_s...  23.5 us
    unnamed x8, local copies, waits for them, and re-layouts  4.44 us
  transfers between devices with their start and end apart: 2, of which 2 were waited for; matrix products, arithmetic and copies ran while one was open for 1% of the time, Pallas kernels for 0%

profile of v1, /device:TPU:0, one launch (start us, length us, event | category | flops | bytes accessed | tf_op | source)
XLA Modules:
  0.0 147.0 jit_solution(5962615528577252038)
XLA Ops:
  6.5 0.0 all-gather.3.cloned.1.call-start
  6.5 0.7 all-gather.3.cloned.1.call-update
  7.3 0.0 all-gather.5.cloned.1.call-start
  7.3 0.7 all-gather.5.cloned.1.call-update
  8.0 0.8 copy.8.vb
  8.8 0.8 copy.9.so
  9.5 53.1 %all-gather.3.cloned.1.call-done.k_ref = bf16[2048,1024]{1,0:T(8,128)(2,1)} async-done(((bf16[128,1024]{1,0:T(8,128)(2,1)}), bf16[2048,1024]{1,0:T(8,128)(2,1)}) %all-gather.3.cloned.1.call-update) | async-done | bytes 4194320 | tf_op jit(solution)/shard_map/all_gather | solution.py:75
  62.6 51.1 %all-gather.5.cloned.1.call-done.v_ref = bf16[2048,1024]{1,0:T(8,128)(2,1)} async-done(((bf16[128,1024]{1,0:T(8,128)(2,1)}), bf16[2048,1024]{1,0:T(8,128)(2,1)}) %all-gather.5.cloned.1.call-update) | async-done | bytes 4194320 | tf_op jit(solution)/shard_map/all_gather | solution.py:76
  113.7 0.0 copy-start
  113.7 1.6 %copy-done = bf16[128,8192]{1,0:T(8,128)(2,1)S(1)} copy-done((bf16[128,8192]{1,0:T(8,128)(2,1)S(1)}, bf16[128,8192]{1,0:T(8,128)(2,1)}, u32[]{:S(2)}) %copy-start) | copy-done | bytes 2097176
  115.3 0.0 copy-start.1
  115.3 0.7 copy-done.1
  116.0 0.0 copy-start.2
  116.0 0.7 copy-done.2
  116.6 23.5 %shard_map.73 = bf16[128,8192]{1,0:T(8,128)(2,1)} custom-call(s32[64,2]{1,0:T(8,128)S(1)} %copy.8.vb, s32[64]{0:T(128)S(1)} %copy-done.1, s32[64,2]{1,0:T(8,128)S(1)} %copy.9.so, s32[64]{0:T(128)S(1)} %copy-done.2, bf16[128,8192]{1,0:T(8,128)(2,1)S(1)} %copy-done, bf16[2048,1024]{1,0:T(8,128)(2,1)} %all-gather.3.cloned.1.call-done.k_ref, ...), custom_call_target="tpu_custom_call" | custom-call | tf_op jit(solution)/shard_map/pallas_call | solution.py:79
Async XLA Ops:
  6.5 56.1 %all-gather.3.cloned.1.call-start = ((), (), s32[]{:S(2)}) async-start(), calls=%async_computation | async-start | bytes 4456448 | tf_op jit(solution)/shard_map/all_gather | solution.py:75
  7.3 106.5 %all-gather.5.cloned.1.call-start = ((), (), s32[]{:S(2)}) async-start(), calls=%async_computation.1 | async-start | bytes 4456448 | tf_op jit(solution)/shard_map/all_gather | solution.py:76
  113.7 1.6 %copy-start = (bf16[128,8192]{1,0:T(8,128)(2,1)S(1)}, bf16[128,8192]{1,0:T(8,128)(2,1)}, u32[]{:S(2)}) copy-start(bf16[128,8192]{1,0:T(8,128)(2,1)} %q_ref.1) | copy-start | bytes 6291460
  115.3 0.7 copy-start.1
  116.0 0.7 copy-start.2
Sparse Core Ops, SparseCore 0:
  9.5 53.0 all-gather.2
  64.8 48.8 all-gather.4

commit v2 on v1

--- a/solution.py
+++ b/solution.py
@@ -10,6 +10,8 @@
 
 HEAD_SIZE = 128
 BLOCK = 128
+SKEW = 2
+PARTS = 2
 
 
 def attend(q, block, head, load_key, load_value, vb, vc, so, sc, causal):
@@ -47,24 +49,189 @@
     return (numerator / total).astype(jnp.bfloat16)
 
 
-def kernel(per_group, vb, vc, so, sc, q_ref, k_ref, v_ref, o_ref):
-    rank = lax.axis_index("seq") * lax.axis_size("tp") + lax.axis_index("tp")
-    group = pl.program_id(0)
-    per_shard = q_ref.shape[0] // BLOCK
+def kernel(
+    n, cores, per_group, slots, vb, vc, so, sc, q_hbm, k_hbm, v_hbm, o_hbm, *scratch
+):
+    kv = scratch[:slots]
+    (q_buf, o_buf, loc_sem, sib_send, sib_recv, q_loc, q_send, q_recv,
+     ring_send, ring_recv, o_loc, o_send, o_recv) = scratch[slots:]
+    rank = lax.axis_index("seq")
+    core = lax.axis_index("tp")
+    other = 1 - core
+    per_shard = q_hbm.shape[0] // BLOCK
+    chip_blocks = cores * per_shard
+    half = n // 2
+    wide = per_group * HEAD_SIZE
+
+    def at_position(p):
+        p = lax.rem(p + n, n)
+        late = p // half
+        return (1 - late) * 2 * p + late * (2 * (n - 1 - p) + 1)
+
+    odd = lax.rem(rank, 2)
+    place = (1 - odd) * (rank // 2) + odd * (n - 1 - rank // 2)
+    ahead, behind = at_position(place + 1), at_position(place - 1)
+
+    barrier = pltpu.get_barrier_semaphore()
+    for peer in ({"seq": ahead}, {"seq": behind}, {"tp": other}):
+        pl.semaphore_signal(
+            barrier, inc=1, device_id=peer, device_id_type=pl.DeviceIdType.MESH
+        )
+
+    def columns(owner, h, width):
+        return pl.ds(pl.multiple_of((owner * slots + h) * width, width), width)
+
+    def remote(src, dst, send, recv, peer):
+        return pltpu.make_async_remote_copy(
+            src_ref=src, dst_ref=dst, send_sem=send, recv_sem=recv,
+            device_id=peer, device_id_type=pl.DeviceIdType.MESH,
+        )
+
+    def kv_local(h, which, b):
+        source = (k_hbm, v_hbm)[which]
+        spot = (rank * cores + core) * per_shard + b
+        return pltpu.make_async_copy(
+            source.at[pl.ds(b * BLOCK, BLOCK), columns(core, h, HEAD_SIZE)],
+            kv[h].at[spot, which],
+            loc_sem.at[h, which, b],
+        )
+
+    def kv_sibling(h, which, b, origin):
+        source = (k_hbm, v_hbm)[which]
+        spot = (rank * cores + origin) * per_shard + b
+        return remote(
+            source.at[pl.ds(b * BLOCK, BLOCK), columns(other, h, HEAD_SIZE)],
+            kv[h].at[spot, which],
+            sib_send.at[h, which, b], sib_recv.at[h, which, b], {"tp": other},
+        )
+
+    def q_local(h):
+        return pltpu.make_async_copy(
+            q_hbm.at[:, columns(core, h, wide)], q_buf.at[h, core], q_loc.at[h]
+        )
+
+    def q_sibling(h, origin):
+        return remote(
+            q_hbm.at[:, columns(other, h, wide)], q_buf.at[h, origin],
+            q_send.at[h], q_recv.at[h], {"tp": other},
+        )
+
+    def hops(h, way):
+        longer = half if h % 2 == way else n - 1 - half
+        return longer
+
+    def ring(h, way, j, incoming):
+        step = 1 - 2 * way
+        origin = place - step * (j if incoming else j - 1)
+        chunk = kv[h].at[pl.ds(at_position(origin) * chip_blocks, chip_blocks)]
+        peer = {"seq": (ahead, behind)[way]}
+        return remote(
+            chunk, chunk, ring_send.at[way, h, j - 1], ring_recv.at[way, h, j - 1], peer
+        )
+
+    pieces = [(which, b) for which in range(2) for b in range(per_shard)]
+    for h in range(slots):
+        for which, b in pieces:
+            kv_local(h, which, b).start()
+        q_local(h).start()
+    pl.semaphore_wait(barrier, 3)
+    for h in range(slots):
+        for which, b in pieces:
+            kv_sibling(h, which, b, core).start()
+    for h in range(slots):
+        q_sibling(h, core).start()
+
+    def tick(t):
+        for h in range(slots):
+            j = t - SKEW * h
+            if j == 1:
+                for which, b in pieces:
+                    kv_local(h, which, b).wait()
+                    kv_sibling(h, which, b, other).wait_recv()
+            for way in range(2):
+                if 2 <= j <= hops(h, way) + 1:
+                    ring(h, way, j - 1, True).wait_recv()
+                if 1 <= j <= hops(h, way):
+                    ring(h, way, j, False).start()
+
     rows = lax.broadcasted_iota(jnp.int32, (BLOCK, BLOCK), 0)
     causal = rows >= lax.broadcasted_iota(jnp.int32, (BLOCK, BLOCK), 1)
-    for b in range(per_shard):
-        span = slice(b * BLOCK, (b + 1) * BLOCK)
-        for slot in range(per_group):
-            cols = slice(slot * HEAD_SIZE, (slot + 1) * HEAD_SIZE)
-            o_ref[span, cols] = attend(
-                q_ref[span, cols],
-                rank * per_shard + b,
-                group * per_group + slot,
-                lambda t: k_ref[pl.ds(pl.multiple_of(t * BLOCK, BLOCK), BLOCK), :],
-                lambda t: v_ref[pl.ds(pl.multiple_of(t * BLOCK, BLOCK), BLOCK), :],
-                vb, vc, so, sc, causal,
-            )
+    share = per_group // PARTS
+    narrow = share * HEAD_SIZE
+
+    def compute(h, part):
+        def one(slot):
+            cols = pl.ds(pl.multiple_of(slot * HEAD_SIZE, HEAD_SIZE), HEAD_SIZE)
+            for c in range(cores):
+                for b in range(per_shard):
+                    span = slice(b * BLOCK, (b + 1) * BLOCK)
+                    o_buf[h, c, span, cols] = attend(
+                        q_buf[h, c, span, cols],
+                        (rank * cores + c) * per_shard + b,
+                        (core * slots + h) * per_group + slot,
+                        lambda t: kv[h][t, 0],
+                        lambda t: kv[h][t, 1],
+                        vb, vc, so, sc, causal,
+                    )
+
+        @pl.loop(part * share, (part + 1) * share)
+        def _(slot):
+            one(slot)
+
+    def out_columns(h, part):
+        start = (core * slots + h) * wide + part * narrow
+        return pl.ds(pl.multiple_of(start, narrow), narrow)
+
+    def out_local(h, part):
+        return pltpu.make_async_copy(
+            o_buf.at[h, core, :, pl.ds(part * narrow, narrow)],
+            o_hbm.at[:, out_columns(h, part)],
+            o_loc.at[h, part],
+        )
+
+    def out_sibling(h, part, incoming):
+        owner = other if incoming else core
+        start = (owner * slots + h) * wide + part * narrow
+        return remote(
+            o_buf.at[h, other, :, pl.ds(part * narrow, narrow)],
+            o_hbm.at[:, pl.ds(pl.multiple_of(start, narrow), narrow)],
+            o_send.at[h, part], o_recv.at[h, part], {"tp": other},
+        )
+
+    longest = half
+    last_tick = SKEW * (slots - 1) + longest + 1
+    done = 0
+    pending = []
+    for h in range(slots):
+        while done < SKEW * h + longest + 1:
+            done += 1
+            tick(done)
+        q_local(h).wait()
+        q_sibling(h, other).wait_recv()
+        for part in range(PARTS):
+            compute(h, part)
+            for item in pending:
+                out_sibling(*item, False).start()
+                out_local(*item).start()
+            pending = [(h, part)]
+            if done < min(last_tick, SKEW * (h + 1) + longest):
+                done += 1
+                tick(done)
+    for item in pending:
+        out_sibling(*item, False).start()
+        out_local(*item).start()
+    for h in range(slots):
+        for which, b in pieces:
+            kv_sibling(h, which, b, core).wait_send()
+        q_sibling(h, core).wait_send()
+        for way in range(2):
+            for j in range(1, hops(h, way) + 1):
+                ring(h, way, j, False).wait_send()
+    for h in range(slots):
+        for part in range(PARTS):
+            out_local(h, part).wait()
+            out_sibling(h, part, False).wait_send()
+            out_sibling(h, part, True).wait_recv()
 
 
 def shards(queries, keys, values, vertical_blocks, vertical_count, slash_offsets, slash_count):
@@ -72,23 +239,38 @@
     groups = keys.shape[1] // HEAD_SIZE
     per_group = heads // groups
     tokens = queries.shape[0]
-    all_keys = lax.all_gather(keys, ("seq", "tp"), axis=0, tiled=True)
-    all_values = lax.all_gather(values, ("seq", "tp"), axis=0, tiled=True)
+    n, cores = lax.axis_size("seq"), lax.axis_size("tp")
+    slots = groups // cores
+    per_shard = tokens // BLOCK
+    blocks = n * cores * per_shard
     smem = pl.BlockSpec(memory_space=pltpu.SMEM)
-    length = all_keys.shape[0]
+    hbm = pl.BlockSpec(memory_space=pl.ANY)
+    dma = pltpu.SemaphoreType.DMA
     return pl.pallas_call(
-        functools.partial(kernel, per_group),
-        grid=(groups,),
-        in_specs=[smem] * 4
+        functools.partial(kernel, n, cores, per_group, slots),
+        in_specs=[smem] * 4 + [hbm] * 3,
+        out_specs=hbm,
+        out_shape=jax.ShapeDtypeStruct(queries.shape, jnp.bfloat16),
+        scratch_shapes=[pltpu.VMEM((blocks, 2, BLOCK, HEAD_SIZE), jnp.bfloat16)] * slots
         + [
-            pl.BlockSpec((tokens, per_group * HEAD_SIZE), lambda g: (0, g)),
-            pl.BlockSpec((length, HEAD_SIZE), lambda g: (0, g)),
-            pl.BlockSpec((length, HEAD_SIZE), lambda g: (0, g)),
+            pltpu.VMEM((slots, cores, tokens, per_group * HEAD_SIZE), jnp.bfloat16),
+            pltpu.VMEM((slots, cores, tokens, per_group * HEAD_SIZE), jnp.bfloat16),
+            dma((slots, 2, per_shard)),
+            dma((slots, 2, per_shard)),
+            dma((slots, 2, per_shard)),
+            dma((slots,)),
+            dma((slots,)),
+            dma((slots,)),
+            dma((2, slots, n // 2)),
+            dma((2, slots, n // 2)),
+            dma((slots, PARTS)),
+            dma((slots, PARTS)),
+            dma((slots, PARTS)),
         ],
-        out_specs=pl.BlockSpec((tokens, per_group * HEAD_SIZE), lambda g: (0, g)),
-        out_shape=jax.ShapeDtypeStruct(queries.shape, jnp.bfloat16),
-        compiler_params=pltpu.CompilerParams(vmem_limit_bytes=48 * 1024 * 1024),
-    )(vertical_blocks, vertical_count, slash_offsets, slash_count, queries, all_keys, all_values)
+        compiler_params=pltpu.CompilerParams(
+            collective_id=0, has_side_effects=True, vmem_limit_bytes=56 * 1024 * 1024
+        ),
+    )(vertical_blocks, vertical_count, slash_offsets, slash_count, queries, keys, values)
 
 
 def solution(mesh):

time: 147 us -> 77.4 us (0.53)
  waiting for transfers between devices: 106 us -> 0 us
  Pallas kernels: 23.5 us -> 71.3 us
  between operations: 13.4 us -> 0.01 us
    all_gather x2 -> x0, waiting for transfers between devices: 104 us -> none  [the longest x1 53.1 us: shards(): all_keys = lax.all_gather(keys, ('seq', 'tp'), axis=0, tiled=True)]
    pallas_call x1, Pallas kernels: 23.5 us -> 71.3 us  [shards(): pl.pallas_call(functools.partial(kernel, n, cores, per_group, slots), in_...]
    unnamed x8 -> x3, local copies, waits for them, and re-layouts: 4.44 us -> 5.84 us
  transfers between devices with their start and end apart: 2 -> 0, of which waited for: 2 -> 0; matrix products, arithmetic and copies ran while one was open for 1% -> 0% of each run, Pallas kernels for 0% -> 0%
where the time goes in v2:
time: 77.4 us; the launch traced here: 77.1 us
  Pallas kernels  71.3 us (92%)
  local copies, waits for them, and re-layouts  5.84 us (8%)
    pallas_call x1, Pallas kernels, shards(): pl.pallas_call(functools.partial(kernel, n, cores, per_group, slots), in_...  71.3 us
    unnamed x3, local copies, waits for them, and re-layouts  5.84 us

profile of v2, /device:TPU:0, one launch (start us, length us, event | category | flops | bytes accessed | tf_op | source)
XLA Modules:
  0.0 77.1 jit_solution(17234554276673020896)
XLA Ops:
  0.0 1.4 %copy.8.vb = s32[64,2]{1,0:T(8,128)} copy(s32[64,2]{0,1:T(2,128)} %param.10) | data formatting | bytes 1024 | tf_op args[3]
  1.4 1.4 %copy.9.so = s32[64,2]{1,0:T(8,128)} copy(s32[64,2]{0,1:T(2,128)} %param.12) | data formatting | bytes 1024 | tf_op args[5]
  2.7 71.3 %shard_map.73 = bf16[128,8192]{1,0:T(8,128)(2,1)} custom-call(s32[64,2]{1,0:T(8,128)} %copy.8.vb, s32[64]{0:T(128)} %vc.1, s32[64,2]{1,0:T(8,128)} %copy.9.so, s32[64]{0:T(128)} %sc.1, bf16[128,8192]{1,0:T(8,128)(2,1)} %q_hbm.1, bf16[128,1024]{1,0:T(8,128)(2,1)} %k_hbm.1, bf16[128,1024]{1,0:T(8,128)(2,1)} %v_hbm.1), custom_call_target="tpu_custom_call" | custom-call | tf_op jit(solution)/shard_map/pallas_call | solution.py:249
  74.0 3.1 %copy.11 = bf16[128,8192]{1,0:T(8,128)(2,1)} copy(bf16[128,8192]{1,0:T(8,128)(2,1)} %shard_map.73) | data formatting | bytes 4194304

commit v3 on v2

v3 whole, which is shorter than its diff:
```python
import functools
import math

import jax
import jax.numpy as jnp
from jax import lax
from jax.experimental import pallas as pl
from jax.experimental.pallas import tpu as pltpu
from jax.sharding import PartitionSpec as P

HEAD_SIZE = 128
BLOCK = 128
SKEW = 3
PARTS = 4


def select(block, head, vb, vc, so, sc):
    nv, ns = vb.shape[0], so.shape[0]
    count_v, count_s = vc[head], sc[head]
    index, live = [block], []
    verticals = [vb[e, head] for e in range(nv)]
    for e in range(nv):
        index.append(verticals[e])
        live.append(jnp.logical_and(e < count_v, verticals[e] < block))
    for e in range(ns):
        target = block - so[e, head]
        ok = jnp.logical_and(e < count_s, target >= 0)
        for f in range(nv):
            taken = jnp.logical_and(f < count_v, verticals[f] == target)
            ok = jnp.logical_and(ok, jnp.logical_not(taken))
        index.append(jnp.maximum(target, 0))
        live.append(ok)
    return index, live


def score(q, keys, live, causal):
    scores = lax.dot_general(
        q, keys, (((1,), (1,)), ((), ())), preferred_element_type=jnp.float32
    )
    tiles = [jnp.where(causal, scores[:, :BLOCK], -jnp.inf)]
    for t, ok in enumerate(live):
        bias = jnp.where(ok, 0.0, -jnp.inf).astype(jnp.float32)
        tiles.append(scores[:, (t + 1) * BLOCK : (t + 2) * BLOCK] + bias)
    return tiles


def soften(tiles):
    factor = HEAD_SIZE**-0.5 * math.log2(math.e)
    highest = functools.reduce(jnp.maximum, tiles)
    peak = jnp.max(highest, axis=1, keepdims=True) * factor
    weights = [jnp.exp2(t * factor - peak) for t in tiles]
    total = jnp.sum(functools.reduce(jnp.add, weights), axis=1, keepdims=True)
    rounded = jnp.concatenate([w.astype(jnp.bfloat16) for w in weights], axis=1)
    return rounded, total


def kernel(
    n, cores, per_group, slots, vb, vc, so, sc, q_hbm, k_hbm, v_hbm, o_hbm, *scratch
):
    keys, values = scratch[:slots], scratch[slots : 2 * slots]
    (q_buf, o_buf, loc_sem, sib_send, sib_recv, q_loc, q_send, q_recv,
     ring_send, ring_recv, o_loc, o_send, o_recv) = scratch[2 * slots :]
    rank = lax.axis_index("seq")
    core = lax.axis_index("tp")
    other = 1 - core
    per_shard = q_hbm.shape[0] // BLOCK
    half = n // 2
    wide = per_group * HEAD_SIZE

    def at_position(p):
        p = lax.rem(p + n, n)
        late = p // half
        return (1 - late) * 2 * p + late * (2 * (n - 1 - p) + 1)

    odd = lax.rem(rank, 2)
    place = (1 - odd) * (rank // 2) + odd * (n - 1 - rank // 2)
    ahead, behind = at_position(place + 1), at_position(place - 1)

    barrier = pltpu.get_barrier_semaphore()
    for peer in ({"seq": ahead}, {"seq": behind}, {"tp": other}):
        pl.semaphore_signal(
            barrier, inc=1, device_id=peer, device_id_type=pl.DeviceIdType.MESH
        )

    def columns(owner, h, width):
        return pl.ds(pl.multiple_of((owner * slots + h) * width, width), width)

    def remote(src, dst, send, recv, peer):
        return pltpu.make_async_remote_copy(
            src_ref=src, dst_ref=dst, send_sem=send, recv_sem=recv,
            device_id=peer, device_id_type=pl.DeviceIdType.MESH,
        )

    def store(which, h):
        return (keys, values)[which][h]

    def kv_local(h, which, b):
        source = (k_hbm, v_hbm)[which]
        spot = (rank * cores + core) * per_shard + b
        return pltpu.make_async_copy(
            source.at[pl.ds(b * BLOCK, BLOCK), columns(core, h, HEAD_SIZE)],
            store(which, h).at[spot],
            loc_sem.at[h, which, b],
        )

    def kv_sibling(h, which, b, origin):
        source = (k_hbm, v_hbm)[which]
        spot = (rank * cores + origin) * per_shard + b
        return remote(
            source.at[pl.ds(b * BLOCK, BLOCK), columns(other, h, HEAD_SIZE)],
            store(which, h).at[spot],
            sib_send.at[h, which, b], sib_recv.at[h, which, b], {"tp": other},
        )

    def q_local(h):
        return pltpu.make_async_copy(
            q_hbm.at[:, columns(core, h, wide)], q_buf.at[h, core], q_loc.at[h]
        )

    def q_sibling(h, origin):
        return remote(
            q_hbm.at[:, columns(other, h, wide)], q_buf.at[h, origin],
            q_send.at[h], q_recv.at[h], {"tp": other},
        )

    def hops(h, way):
        return half if h % 2 == way else n - 1 - half

    def ring(h, way, j, piece, incoming):
        whose, which = piece
        step = 1 - 2 * way
        origin = place - step * (j if incoming else j - 1)
        spot = (at_position(origin) * cores + (core, other)[whose]) * per_shard
        chunk = store(which, h).at[pl.ds(spot, per_shard)]
        sem = (way, h, j - 1, 2 * whose + which)
        peer = {"seq": (ahead, behind)[way]}
        return remote(chunk, chunk, ring_send.at[sem], ring_recv.at[sem], peer)

    ring_pieces = [(whose, which) for whose in range(2) for which in range(2)]
    pieces = [(which, b) for which in range(2) for b in range(per_shard)]
    for h in range(slots):
        for which, b in pieces:
            kv_local(h, which, b).start()
    for h in range(slots):
        q_local(h).start()
    pl.semaphore_wait(barrier, 3)
    for h in range(slots):
        for which, b in pieces:
            kv_sibling(h, which, b, core).start()
    for h in range(slots):
        q_sibling(h, core).start()

    def event(h, way, j, piece):
        whose, which = piece
        if j == 1 and way == 0:
            for b in range(per_shard):
                if whose == 0:
                    kv_local(h, which, b).wait()
                else:
                    kv_sibling(h, which, b, other).wait_recv()
        if j >= 2:
            ring(h, way, j - 1, piece, True).wait_recv()
        if j <= hops(h, way):
            ring(h, way, j, piece, False).start()

    events, ready = [], []
    for t in range(1, SKEW * (slots - 1) + half + 2):
        for h in range(slots):
            j = t - SKEW * h
            for piece in ring_pieces:
                for way in range(2):
                    if 1 <= j <= hops(h, way) + 1:
                        events.append((h, way, j, piece))
            if j == half + 1:
                ready.append(len(events))

    rows = lax.broadcasted_iota(jnp.int32, (BLOCK, BLOCK), 0)
    causal = rows >= lax.broadcasted_iota(jnp.int32, (BLOCK, BLOCK), 1)

    def compute(h, slot, units):
        cols = slice(slot * HEAD_SIZE, (slot + 1) * HEAD_SIZE)
        head = (core * slots + h) * per_group + slot
        chosen = [
            select((rank * cores + c) * per_shard + b, head, vb, vc, so, sc)
            for c, b in units
        ]
        spans = [(c, slice(b * BLOCK, (b + 1) * BLOCK)) for c, b in units]
        tiles = [
            score(
                q_buf[h, c, span, cols],
                jnp.concatenate([keys[h][t] for t in index], axis=0),
                live,
                causal,
            )
            for (c, span), (index, live) in zip(spans, chosen)
        ]
        softened = [soften(t) for t in tiles]
        for (c, span), (index, _), (rounded, total) in zip(spans, chosen, softened):
            vals = jnp.concatenate([values[h][t] for t in index], axis=0)
            numerator = jnp.dot(rounded, vals, preferred_element_type=jnp.float32)
            o_buf[h, c, span, cols] = (numerator / total).astype(jnp.bfloat16)

    share = per_group // PARTS
    narrow = share * HEAD_SIZE

    def out_columns(owner, h, part):
        start = (owner * slots + h) * wide + part * narrow
        return pl.ds(pl.multiple_of(start, narrow), narrow)

    def out_local(h, part):
        return pltpu.make_async_copy(
            o_buf.at[h, core, :, pl.ds(part * narrow, narrow)],
            o_hbm.at[:, out_columns(core, h, part)],
            o_loc.at[h, part],
        )

    def out_sibling(h, part, incoming):
        return remote(
            o_buf.at[h, other, :, pl.ds(part * narrow, narrow)],
            o_hbm.at[:, out_columns(other if incoming else core, h, part)],
            o_send.at[h, part], o_recv.at[h, part], {"tp": other},
        )

    units = [(c, b) for c in range(cores) for b in range(per_shard)]
    done = 0
    pending = []
    for h in range(slots):
        while done < ready[h]:
            event(*events[done])
            done += 1
        q_local(h).wait()
        q_sibling(h, other).wait_recv()
        first = done
        rest = (ready[h + 1] if h + 1 < slots else len(events)) - first
        for slot in range(per_group):
            while done < first + rest * (slot + 1) // per_group:
                event(*events[done])
                done += 1
            compute(h, slot, units)
            if slot % share == share - 1:
                for item in pending:
                    out_sibling(*item, False).start()
                    out_local(*item).start()
                pending = [(h, slot // share)]
    for item in pending:
        out_sibling(*item, False).start()
        out_local(*item).start()
    for h in range(slots):
        for which, b in pieces:
            kv_sibling(h, which, b, core).wait_send()
        q_sibling(h, core).wait_send()
        for way in range(2):
            for j in range(1, hops(h, way) + 1):
                for piece in ring_pieces:
                    ring(h, way, j, piece, False).wait_send()
    for h in range(slots):
        for part in range(PARTS):
            out_local(h, part).wait()
            out_sibling(h, part, False).wait_send()
            out_sibling(h, part, True).wait_recv()


def shards(queries, keys, values, vertical_blocks, vertical_count, slash_offsets, slash_count):
    heads = vertical_count.shape[0]
    groups = keys.shape[1] // HEAD_SIZE
    per_group = heads // groups
    tokens = queries.shape[0]
    n, cores = lax.axis_size("seq"), lax.axis_size("tp")
    slots = groups // cores
    per_shard = tokens // BLOCK
    blocks = n * cores * per_shard
    smem = pl.BlockSpec(memory_space=pltpu.SMEM)
    hbm = pl.BlockSpec(memory_space=pl.ANY)
    dma = pltpu.SemaphoreType.DMA
    return pl.pallas_call(
        functools.partial(kernel, n, cores, per_group, slots),
        in_specs=[smem] * 4 + [hbm] * 3,
        out_specs=hbm,
        out_shape=jax.ShapeDtypeStruct(queries.shape, jnp.bfloat16),
        scratch_shapes=[pltpu.VMEM((blocks, BLOCK, HEAD_SIZE), jnp.bfloat16)] * (2 * slots)
        + [
            pltpu.VMEM((slots, cores, tokens, per_group * HEAD_SIZE), jnp.bfloat16),
            pltpu.VMEM((slots, cores, tokens, per_group * HEAD_SIZE), jnp.bfloat16),
            dma((slots, 2, per_shard)),
            dma((slots, 2, per_shard)),
            dma((slots, 2, per_shard)),
            dma((slots,)),
            dma((slots,)),
            dma((slots,)),
            dma((2, slots, n // 2, 4)),
            dma((2, slots, n // 2, 4)),
            dma((slots, PARTS)),
            dma((slots, PARTS)),
            dma((slots, PARTS)),
        ],
        compiler_params=pltpu.CompilerParams(
            collective_id=0, has_side_effects=True, vmem_limit_bytes=56 * 1024 * 1024
        ),
    )(vertical_blocks.T, vertical_count, slash_offsets.T, slash_count, queries, keys, values)


def solution(mesh):
    rows = P(("groups", "seq", "tp"), None)
    return jax.shard_map(
        shards,
        mesh=mesh,
        in_specs=(rows, rows, rows, P(), P(), P(), P()),
        out_specs=rows,
        check_vma=False,
    )
```

time: 77.4 us -> 69.1 us (0.89)
  Pallas kernels: 71.3 us -> 65.8 us
  local copies, waits for them, and re-layouts: 5.84 us -> 3.1 us
    pallas_call x1, Pallas kernels: 71.3 us -> 65.8 us  [shards(): pl.pallas_call(functools.partial(kernel, n, cores, per_group, slots), in_...]
    unnamed x3 -> x1, local copies, waits for them, and re-layouts: 5.84 us -> 3.1 us
where the time goes in v3:
time: 69.1 us; the launch traced here: 68.9 us
  Pallas kernels  65.8 us (95%)
  local copies, waits for them, and re-layouts  3.1 us (4%)
    pallas_call x1, Pallas kernels, shards(): pl.pallas_call(functools.partial(kernel, n, cores, per_group, slots), in_...  65.8 us
    unnamed x1, local copies, waits for them, and re-layouts  3.1 us

profile of v3, /device:TPU:0, one launch (start us, length us, event | category | flops | bytes accessed | tf_op | source)
XLA Modules:
  0.0 68.9 jit_solution(4940896837385540739)
XLA Ops:
  0.0 65.8 %shard_map.73 = bf16[128,8192]{1,0:T(8,128)(2,1)} custom-call(s32[2,64]{1,0:T(2,128)} %bitcast.2, s32[64]{0:T(128)} %vc.1, s32[2,64]{1,0:T(2,128)} %bitcast.3, s32[64]{0:T(128)} %sc.1, bf16[128,8192]{1,0:T(8,128)(2,1)} %q_hbm.1, bf16[128,1024]{1,0:T(8,128)(2,1)} %k_hbm.1, bf16[128,1024]{1,0:T(8,128)(2,1)} %v_hbm.1), custom_call_target="tpu_custom_call" | custom-call | tf_op jit(solution)/shard_map/pallas_call | solution.py:275
  65.9 3.1 %copy.9 = bf16[128,8192]{1,0:T(8,128)(2,1)} copy(bf16[128,8192]{1,0:T(8,128)(2,1)} %shard_map.73) | data formatting | bytes 4194304

commit v4 on v3

--- a/solution.py
+++ b/solution.py
@@ -10,7 +10,7 @@
 
 HEAD_SIZE = 128
 BLOCK = 128
-SKEW = 3
+SKEW = 1
 PARTS = 4
 
 
@@ -163,10 +163,13 @@
         if j <= hops(h, way):
             ring(h, way, j, piece, False).start()
 
+    def start(h):
+        return h * SKEW
+
     events, ready = [], []
-    for t in range(1, SKEW * (slots - 1) + half + 2):
+    for t in range(1, start(slots - 1) + half + 2):
         for h in range(slots):
-            j = t - SKEW * h
+            j = t - start(h)
             for piece in ring_pieces:
                 for way in range(2):
                     if 1 <= j <= hops(h, way) + 1:

time: 69.1 us -> 61.4 us (0.89)
  Pallas kernels: 65.8 us -> 58.1 us
    pallas_call x1, Pallas kernels: 65.8 us -> 58.1 us  [shards(): pl.pallas_call(functools.partial(kernel, n, cores, per_group, slots), in_...]
where the time goes in v4:
time: 61.4 us; the launch traced here: 61.2 us
  Pallas kernels  58.1 us (95%)
  local copies, waits for them, and re-layouts  3.1 us (5%)
    pallas_call x1, Pallas kernels, shards(): pl.pallas_call(functools.partial(kernel, n, cores, per_group, slots), in_...  58.1 us
    unnamed x1, local copies, waits for them, and re-layouts  3.1 us

profile of v4, /device:TPU:0, one launch (start us, length us, event | category | flops | bytes accessed | tf_op | source)
XLA Modules:
  0.0 61.2 jit_solution(1072309025508894287)
XLA Ops:
  0.0 58.1 %shard_map.73 = bf16[128,8192]{1,0:T(8,128)(2,1)} custom-call(s32[2,64]{1,0:T(2,128)} %bitcast.2, s32[64]{0:T(128)} %vc.1, s32[2,64]{1,0:T(2,128)} %bitcast.3, s32[64]{0:T(128)} %sc.1, bf16[128,8192]{1,0:T(8,128)(2,1)} %q_hbm.1, bf16[128,1024]{1,0:T(8,128)(2,1)} %k_hbm.1, bf16[128,1024]{1,0:T(8,128)(2,1)} %v_hbm.1), custom_call_target="tpu_custom_call" | custom-call | tf_op jit(solution)/shard_map/pallas_call | solution.py:278
  58.1 3.1 %copy.9 = bf16[128,8192]{1,0:T(8,128)(2,1)} copy(bf16[128,8192]{1,0:T(8,128)(2,1)} %shard_map.73) | data formatting | bytes 4194304
